TPU v7x, 32 devices: a whole 2x2x4 slice. The times are simulated.
32 devices in a mesh: dp: 16 (over z, y, x), grp: 2 (over core).
Axes of the slice: x: 2, y: 2, z: 4, core: 2. Of those that a mesh axis runs over, the one named last changes fastest.
Arguments:
- embeds: bfloat16 [8192, 1024], P(('dp', 'grp')), may hold values from -7 to 7
- quality: float32 [8192], P(('dp', 'grp')), may hold values from 0.5 to 2
- domain_ids: int32 [8192], P(('dp', 'grp')), may hold values from 0 to 15, as said below
- domain_weight: float32 [16], replicated, may hold values from 0.5 to 2
- dest: int32 [8192], P(('dp', 'grp')), may hold values from 0 to 31, as said below
- counts: int32 [32], P(('dp', 'grp')), may hold values from 192 to 256, as said below
- winners: int32 [4], replicated, may hold values from 0 to 8191, as said below
Outputs:
- relaid: bfloat16 [16384, 1024], P(('dp', 'grp'))
- residual_gain: float32 [16384], P(('dp', 'grp'))
- chol_rows: float32 [4, 16384], P(None, ('dp', 'grp'))
Inputs may be any that keep to these rules, and one draw needn't show every extreme that they name: Rows 0 to counts - 1 of a device are valid, and one device has 256 valid rows. `dest`: destination device over dp and grp (index over dp+grp); among the valid rows of one device at most 16 name any one destination, and on every device some destination is named by exactly 16 valid rows. `domain_ids`: non-decreasing within each device's rows; a device's rows carry one domain number or two consecutive ones. `winners`: distinct valid rows, on distinct devices.
All inputs are finite; a program needn't handle non-finite values.
Results may differ from a plain program's by a relative error of at most 0.0048.
The roundings to bfloat16 on the way count: a program that leaves them out, or rounds other values in their place, can miss the bound.
Values may be sent and summed in bfloat16 or wider, within the bound.
A program may use at most 64 MiB of HBM per device.

v0:
```python
import jax
import jax.numpy as jnp
from jax import lax
from jax.sharding import PartitionSpec as P

RIDGE = 0.1


def body(embeds, quality, domain_ids, domain_weight, dest, counts, winners):
    shards = lax.axis_size(("dp", "grp"))
    pair_size = lax.axis_size("grp")
    spread_size = lax.axis_size("dp")
    slot_count = embeds.shape[0]
    feature_width = embeds.shape[1]
    step_count = winners.shape[0]
    domains = domain_weight.shape[0]
    per_pair = 2 * slot_count // shards
    balanced = shards * per_pair
    source = lax.axis_index(("dp", "grp"))
    row_index = jnp.arange(slot_count, dtype=jnp.int32)
    is_valid = row_index < counts[0]
    matches = domain_ids[:, None] == jnp.arange(domains, dtype=jnp.int32)[None, :]
    weight_row = jnp.sum(jnp.where(matches, domain_weight[None, :], 0.0), axis=1)
    row_quality = jnp.where(is_valid, quality * weight_row, 0.0).astype(jnp.bfloat16)
    targets = jnp.arange(shards, dtype=jnp.int32)
    dest_hot = ((dest[:, None] == targets[None, :]) & is_valid[:, None]).astype(jnp.bfloat16)
    strictly_lower = (row_index[None, :] < row_index[:, None]).astype(jnp.bfloat16)
    earlier_count = jnp.dot(strictly_lower, dest_hot, preferred_element_type=jnp.float32)
    dest_rank = jnp.sum(jnp.where(dest_hot > 0, earlier_count, 0.0), axis=1).astype(jnp.int32)
    send_slot = jnp.where(is_valid, dest * per_pair + dest_rank, balanced)
    bal_place = (dest * balanced + source * per_pair + dest_rank).astype(jnp.float32)
    send_rows = (
        jnp.zeros((balanced, feature_width), jnp.bfloat16).at[send_slot].set(embeds, mode="drop")
    )
    send_rows = send_rows.reshape(spread_size, pair_size, per_pair, feature_width)
    send_quality = jnp.zeros((balanced,), jnp.bfloat16).at[send_slot].set(row_quality, mode="drop")
    send_quality = send_quality.reshape(spread_size, pair_size, per_pair)
    quality_wide = row_quality.astype(jnp.float32)
    first_hop = (
        lax.all_to_all(send_rows, "dp", split_axis=0, concat_axis=0, tiled=True),
        lax.all_to_all(send_quality, "dp", split_axis=0, concat_axis=0, tiled=True),
    )
    rows_in = lax.all_to_all(first_hop[0], "grp", split_axis=1, concat_axis=1, tiled=True)
    quality_in = lax.all_to_all(first_hop[1], "grp", split_axis=1, concat_axis=1, tiled=True)
    row_norms = jnp.einsum("abmd,abmd->abm", rows_in, rows_in, preferred_element_type=jnp.float32)
    relaid = rows_in.reshape(balanced, feature_width)
    bal_quality = quality_in.reshape(balanced).astype(jnp.float32)
    row_norms = row_norms.reshape(balanced)
    residual_gain = jnp.where(
        bal_quality > 0, bal_quality * bal_quality * row_norms / feature_width + RIDGE, 0.0
    )
    local_place = (source * balanced + jnp.arange(balanced, dtype=jnp.int32)).astype(jnp.float32)
    kept_rows = []
    kept_quality = []
    kept_columns = []
    kept_roots = []
    chol_list = []
    for turn_index in range(step_count):
        chosen = (
            row_index[None, :]
            == (winners[turn_index : turn_index + 1] - source * slot_count)[:, None]
        )
        picked_rows = jnp.dot(
            chosen.astype(jnp.bfloat16), embeds, preferred_element_type=jnp.float32
        )
        picked_quality = jnp.sum(jnp.where(chosen, quality_wide[None, :], 0.0), axis=1)
        picked_place = jnp.sum(jnp.where(chosen, bal_place[None, :], 0.0), axis=1)
        row_sum, quality_sum, place_sum = lax.psum(
            (picked_rows, picked_quality, picked_place), ("dp", "grp")
        )
        row_now = row_sum[0].astype(jnp.bfloat16)
        quality_now = quality_sum[0]
        place_now = place_sum[0]
        dot_now = jnp.dot(relaid, row_now, preferred_element_type=jnp.float32)
        column_now = []
        for prior_step in range(turn_index):
            cross_term = (
                kept_quality[prior_step]
                * quality_now
                * jnp.dot(kept_rows[prior_step], row_now, preferred_element_type=jnp.float32)
                / feature_width
            )
            for earlier in range(prior_step):
                cross_term = cross_term - kept_columns[prior_step][earlier] * column_now[earlier]
            column_now.append(cross_term / kept_roots[prior_step])
        self_term = (
            quality_now
            * quality_now
            * jnp.dot(row_now, row_now, preferred_element_type=jnp.float32)
            / feature_width
            + RIDGE
        )
        for prior_step in range(turn_index):
            self_term = self_term - column_now[prior_step] * column_now[prior_step]
        root_now = jnp.sqrt(self_term)
        inner_sum = jnp.zeros_like(residual_gain)
        for prior_step in range(turn_index):
            inner_sum = inner_sum + chol_list[prior_step] * column_now[prior_step]
        ridge_hit = jnp.where(local_place == place_now, RIDGE, 0.0)
        new_entry = (
            bal_quality * quality_now * dot_now / feature_width + ridge_hit - inner_sum
        ) / root_now
        chol_list.append(new_entry)
        residual_gain = residual_gain - new_entry * new_entry
        kept_rows.append(row_now)
        kept_quality.append(quality_now)
        kept_columns.append(column_now)
        kept_roots.append(root_now)
    return (relaid, residual_gain, jnp.stack(chol_list))


def solution(mesh):
    return jax.shard_map(
        body,
        mesh=mesh,
        in_specs=(
            P(("dp", "grp"), None),
            P(("dp", "grp")),
            P(("dp", "grp")),
            P(),
            P(("dp", "grp")),
            P(("dp", "grp")),
            P(),
        ),
        out_specs=(P(("dp", "grp"), None), P(("dp", "grp")), P(None, ("dp", "grp"))),
        check_vma=False,
    )
```

profile of v0, /device:TPU:0, one launch (start us, length us, event | category | flops | bytes accessed | tf_op | source)
XLA Modules:
  0.0 117.8 jit_solution(18010897146661138979)
XLA Ops:
  0.6 1.4 %fusion.41 = (s32[1]{0:T(128)}, s32[1]{0:T(128)}, s32[1]{0:T(128)}, s32[1]{0:T(128)}) fusion(s32[4]{0:T(128)} %param.13), kind=kLoop, calls=%fused_computation.95 | loop fusion | bytes 32 | tf_op jit(solution)/shard_map/slice | solution.py:61
  5.2 1.0 fusion.1
  6.2 0.8 select_reduce_fusion
  6.9 0.7 add_add_fusion
  7.6 1.4 %fusion.38 = (f32[]{:T(128)}, f32[]{:T(128)}, f32[]{:T(128)}, f32[]{:T(128)}, bf16[256]{0:T(256)(128)(2,1)S(1)}) fusion(s32[]{:T(128)} %bitcast.13, s32[]{:T(128)} %bitcast.7, s32[]{:T(128)} %bitcast.10, s32[]{:T(128)} %bitcast.4, f32[256]{0:T(256)} %param.8, f32[256]{0:T(256)S(1)} %select_reduce_fusion, s32[]{:T(128)} %bitcast.50), kind=kLoop, calls=%fused_computation.81 | loop fusion | flops 4348 | bytes 2596 | tf_op jit(solution)/shard_map/reduce_sum | solution.py:66
  9.0 2.2 %scatter_custom_fusion.1 = bf16[512]{0:T(512)(128)(2,1)S(1)} fusion(s32[256]{0:T(256)S(1)} %get-tuple-element.45, bf16[256]{0:T(256)(128)(2,1)S(1)} %get-tuple-element.38, bf16[]{:T(256)} %constant.18.clone.1), kind=kCustom, calls=%fused_computation.93 | custom fusion | bytes 1026 | tf_op jit(solution)/shard_map/scatter | solution.py:36
  11.2 0.7 reshape.113
  11.9 8.3 %all-to-all-start.2 = ((bf16[16,2,16]{2,1,0:T(2,128)(2,1)}), bf16[16,2,16]{2,1,0:T(2,128)(2,1)S(1)}, u32[]{:S(2)}, u32[]{:S(2)}) async-start(bf16[16,2,16]{2,1,0:T(2,128)(2,1)} %reshape.113), calls=%async_computation.2 | async-start | bytes 16384 | tf_op jit(solution)/shard_map/all_to_all | solution.py:41
  20.2 3.1 %scatter_custom_fusion = bf16[512,1024]{1,0:T(8,128)(2,1)} fusion(s32[256]{0:T(256)S(1)} %get-tuple-element.45, bf16[256,1024]{1,0:T(8,128)(2,1)} %param.7, bf16[]{:T(256)} %constant.18.clone.1), kind=kCustom, calls=%fused_computation.6 | custom fusion | bytes 1049088 | tf_op jit(solution)/shard_map/scatter | solution.py:33
  23.3 4.1 %all-to-all-done.2 = bf16[16,2,16]{2,1,0:T(2,128)(2,1)S(1)} async-done(((bf16[16,2,16]{2,1,0:T(2,128)(2,1)}), bf16[16,2,16]{2,1,0:T(2,128)(2,1)S(1)}, u32[]{:S(2)}, u32[]{:S(2)}) %all-to-all-start.2) | async-done | bytes 1056 | tf_op jit(solution)/shard_map/all_to_all | solution.py:41
  27.4 0.1 reshape.204
  27.5 3.7 %all_to_all.20 = bf16[2,2,128]{2,1,0:T(2,128)(2,1)S(1)} all-to-all(bf16[2,2,128]{2,1,0:T(2,128)(2,1)S(1)} %reshape.204), channel_id=1, replica_groups=mesh['dp'=16,'grp'=2] {'grp'}, dimensions={0} | all-to-all | bytes 2048 | tf_op jit(solution)/shard_map/all_to_all | solution.py:44
  31.2 3.8 %all-to-all-start = ((bf16[16,2,16,1024]{3,2,1,0:T(8,128)(2,1)}), bf16[16,2,16,1024]{3,2,1,0:T(8,128)(2,1)S(1)}, u32[]{:S(2)}, u32[]{:S(2)}) async-start(bf16[16,2,16,1024]{3,2,1,0:T(8,128)(2,1)} %bitcast.1), calls=%async_computation | async-start | bytes 2097152 | tf_op jit(solution)/shard_map/all_to_all | solution.py:40
  35.1 0.7 select_reduce_fusion.1
  35.8 0.2 fusion.42
  36.0 0.2 fusion.43
  36.1 0.2 fusion.44
  36.3 0.2 fusion.45
  36.5 47.5 %all-reduce = (f32[]{:T(128)}, bf16[1,1024]{1,0:T(2,128)(2,1)S(1)}, bf16[1,1024]{1,0:T(2,128)(2,1)S(1)}, bf16[1,1024]{1,0:T(2,128)(2,1)S(1)}, bf16[1,1024]{1,0:T...) all-reduce(f32[]{:T(128)} %get-tuple-element.20, ...), channel_id=1, replica_groups=mesh['dp'=16,'grp'=2] {'dp','grp'}, use_global_device_ids=true, to_apply=%region_5.6 | all-reduce | flops 4104 | bytes 24640 | tf_op jit(solution)/shard_map/psum | solution.py:68
  91.9 0.7 fusion.17
  104.5 0.1 copy.27
  104.6 4.6 %all_to_all.21 = bf16[16,2,16,1024]{3,2,0,1:T(8,128)(2,1)S(1)} all-to-all(bf16[16,2,16,1024]{3,2,0,1:T(8,128)(2,1)S(1)} %copy.27), channel_id=1, replica_groups=mesh['dp'=16,'grp'=2] {'grp'}, dimensions={1} | all-to-all | bytes 2097152 | tf_op jit(solution)/shard_map/all_to_all | solution.py:43
  109.1 0.1 copy.28
  109.3 0.4 fusion.29
  109.6 0.4 fusion.27
  110.0 0.4 fusion.25
  110.4 0.4 fusion.23
  110.8 0.3 fusion
  111.1 2.6 %convert_multiply_fusion.4 = (f32[16,2,16]{2,0,1:T(8,128)S(1)}, f32[16,2,16]{2,0,1:T(8,128)S(1)}, f32[16,2,16]{2,0,1:T(8,128)S(1)}, f32[16,2,16]{2,0,1:T(8,128)S(1)}, f32[16,2,16]{2,0,1:T(8,128)S(1)}) fusion(f32[]{:T(128)} %get-tuple-element.21, f32[]{:T(128)} %get-tuple-element.27, f32[]{:T(128)} %get-tuple-element.29, f32[]{:T(128)} %get-tuple-element.31, ...), kind=kLoop, calls=%fused_computation.12 | loop fusion | flops 5632 | bytes 13328 | tf_op jit(solution)/shard_map/mul | solution.py:101
  113.7 0.1 mul.230
  114.2 3.0 %multiply_subtract_fusion = (f32[512]{0:T(512)}, f32[512]{0:T(512)S(1)}, f32[512]{0:T(512)S(1)}, f32[512]{0:T(512)S(1)}, f32[512]{0:T(512)S(1)}) fusion(f32[512]{0:T(512)S(1)} %reshape.125, f32[]{:T(128)S(6)} %sqrt.15, f32[]{:T(128)S(6)} %div.115, f32[]{:T(128)S(6)} %div.113, f32[]{:T(128)S(6)} %div.111, f32[]{:T(128)} %get-tuple-element.32, s32[]{:T(128)S(6)} %mul.232, ...), kind=kLoop, calls=%fused_computation.64 | loop fusion | flops 23552 | bytes 28732 | tf_op jit(solution)/shard_map/sub | solution.py:104
  117.2 0.6 pad_maximum_fusion
  (27 shorter events, 0.6 us)
Async XLA Ops:
  11.9 15.6 %all-to-all-start.2 = ((bf16[16,2,16]{2,1,0:T(2,128)(2,1)}), bf16[16,2,16]{2,1,0:T(2,128)(2,1)S(1)}, u32[]{:S(2)}, u32[]{:S(2)}) async-start(bf16[16,2,16]{2,1,0:T(2,128)(2,1)} %reshape.113), calls=%async_computation.2 | async-start | bytes 16384 | tf_op jit(solution)/shard_map/all_to_all | solution.py:41
  31.2 4.6 %copy-start.1 = (bf16[256,1024]{1,0:T(8,128)(2,1)S(1)}, bf16[256,1024]{1,0:T(8,128)(2,1)}, u32[]{:S(2)}) copy-start(bf16[256,1024]{1,0:T(8,128)(2,1)} %param.7) | copy-start | bytes 1572868
  31.2 73.2 %all-to-all-start = ((bf16[16,2,16,1024]{3,2,1,0:T(8,128)(2,1)}), bf16[16,2,16,1024]{3,2,1,0:T(8,128)(2,1)S(1)}, u32[]{:S(2)}, u32[]{:S(2)}) async-start(bf16[16,2,16,1024]{3,2,1,0:T(8,128)(2,1)} %bitcast.1), calls=%async_computation | async-start | bytes 2097152 | tf_op jit(solution)/shard_map/all_to_all | solution.py:40
  109.3 1.2 copy-start
where the time goes:
time: 119 us; the launch traced here: 118 us
  blocking collectives  55.7 us (47%)
  between operations  23.6 us (20%)
  starting transfers between devices  12.1 us (10%)
  other arithmetic  10.7 us (9%)
  local copies, waits for them, and re-layouts  8.38 us (7%)
  waiting for transfers between devices  4.08 us (3%)
  matrix products  3.22 us (3%)
    psum x1, blocking collectives, body(): lax.psum((picked_rows, picked_quality, picked_place), ('dp', 'grp'))  47.5 us
    all_to_all x1, starting transfers between devices, body(): lax.all_to_all(send_quality, 'dp', split_axis=0, concat_axis=0, tiled=True)  8.34 us
    all_to_all x1, blocking collectives, body(): lax.all_to_all(first_hop[0], 'grp', split_axis=1, concat_axis=1, tiled=True)  4.58 us
    all_to_all x1, waiting for transfers between devices, body(): lax.all_to_all(send_quality, 'dp', split_axis=0, concat_axis=0, tiled=True)  4.08 us
    all_to_all x1, starting transfers between devices, body(): lax.all_to_all(send_rows, 'dp', split_axis=0, concat_axis=0, tiled=True)  3.79 us
    all_to_all x1, blocking collectives, body(): lax.all_to_all(first_hop[1], 'grp', split_axis=1, concat_axis=1, tiled=True)  3.69 us
    scatter x1, local copies, waits for them, and re-layouts, body(): jnp.zeros((balanced, feature_width), jnp.bfloat16).at[send_slot]  3.15 us
    sub x1, other arithmetic, body(): residual_gain = residual_gain - new_entry * new_entry  2.97 us
  transfers between devices with their start and end apart: 2, of which 1 were waited for; matrix products, arithmetic and copies ran while one was open for 5% of the time, Pallas kernels for 0%

commit v1 on v0

--- a/solution.py
+++ b/solution.py
@@ -4,6 +4,12 @@
 from jax.sharding import PartitionSpec as P
 
 RIDGE = 0.1
+
+
+def lanes_number(sample):
+    block_next = lax.psum(sample, "grp")
+    side_arr = lax.psum(block_next, "dp")
+    return side_arr
 
 
 def body(embeds, quality, domain_ids, domain_weight, dest, counts, winners):
@@ -65,9 +71,7 @@
         )
         picked_quality = jnp.sum(jnp.where(chosen, quality_wide[None, :], 0.0), axis=1)
         picked_place = jnp.sum(jnp.where(chosen, bal_place[None, :], 0.0), axis=1)
-        row_sum, quality_sum, place_sum = lax.psum(
-            (picked_rows, picked_quality, picked_place), ("dp", "grp")
-        )
+        row_sum, quality_sum, place_sum = lanes_number((picked_rows, picked_quality, picked_place))
         row_now = row_sum[0].astype(jnp.bfloat16)
         quality_now = quality_sum[0]
         place_now = place_sum[0]

time: 119 us -> 158 us (1.33)
  blocking collectives: 55.7 us -> 95.3 us
    psum x1 -> x2, blocking collectives: 47.5 us -> 87.1 us  [the longest x1 82.4 us: lanes_number(): side_arr = lax.psum(block_next, 'dp')]
  transfers between devices with their start and end apart: 2 -> 2, of which waited for: 1 -> 1; matrix products, arithmetic and copies ran while one was open for 5% -> 3% of each run, Pallas kernels for 0% -> 0%
where the time goes in v1:
time: 158 us; the launch traced here: 157 us
  blocking collectives  95.3 us (60%)
  between operations  23.6 us (15%)
  starting transfers between devices  12.1 us (8%)
  other arithmetic  10.7 us (7%)
  local copies, waits for them, and re-layouts  8.38 us (5%)
  waiting for transfers between devices  4.08 us (3%)
  matrix products  3.22 us (2%)
    psum x1, blocking collectives, lanes_number(): side_arr = lax.psum(block_next, 'dp')  82.4 us
    all_to_all x1, starting transfers between devices, body(): lax.all_to_all(send_quality, 'dp', split_axis=0, concat_axis=0, tiled=True)  8.34 us
    psum x1, blocking collectives, lanes_number(): block_next = lax.psum(sample, 'grp')  4.64 us
    all_to_all x1, blocking collectives, body(): lax.all_to_all(first_hop[0], 'grp', split_axis=1, concat_axis=1, tiled=True)  4.58 us
    all_to_all x1, waiting for transfers between devices, body(): lax.all_to_all(send_quality, 'dp', split_axis=0, concat_axis=0, tiled=True)  4.08 us
    all_to_all x1, starting transfers between devices, body(): lax.all_to_all(send_rows, 'dp', split_axis=0, concat_axis=0, tiled=True)  3.79 us
    all_to_all x1, blocking collectives, body(): lax.all_to_all(first_hop[1], 'grp', split_axis=1, concat_axis=1, tiled=True)  3.69 us
  transfers between devices with their start and end apart: 2, of which 1 were waited for; matrix products, arithmetic and copies ran while one was open for 3% of the time, Pallas kernels for 0%

profile of v1, /device:TPU:0, one launch (start us, length us, event | category | flops | bytes accessed | tf_op | source)
XLA Modules:
  0.0 157.4 jit_solution(10076983927141514107)
XLA Ops:
  0.6 1.4 fusion.41
  5.2 1.0 fusion.1
  6.2 0.8 select_reduce_fusion
  6.9 0.7 add_add_fusion
  7.6 1.4 fusion.38
  9.0 2.2 %scatter_custom_fusion.1 = bf16[512]{0:T(512)(128)(2,1)S(1)} fusion(s32[256]{0:T(256)S(1)} %get-tuple-element.57, bf16[256]{0:T(256)(128)(2,1)S(1)} %get-tuple-element.50, bf16[]{:T(256)} %constant.18.clone.1), kind=kCustom, calls=%fused_computation.93 | custom fusion | bytes 1026 | tf_op jit(solution)/shard_map/scatter | solution.py:42
  11.2 0.7 reshape.113
  11.8 8.3 %all-to-all-start.2 = ((bf16[16,2,16]{2,1,0:T(2,128)(2,1)}), bf16[16,2,16]{2,1,0:T(2,128)(2,1)S(1)}, u32[]{:S(2)}, u32[]{:S(2)}) async-start(bf16[16,2,16]{2,1,0:T(2,128)(2,1)} %reshape.113), calls=%async_computation.2 | async-start | bytes 16384 | tf_op jit(solution)/shard_map/all_to_all | solution.py:47
  20.2 3.1 %scatter_custom_fusion = bf16[512,1024]{1,0:T(8,128)(2,1)} fusion(s32[256]{0:T(256)S(1)} %get-tuple-element.57, bf16[256,1024]{1,0:T(8,128)(2,1)} %param.7, bf16[]{:T(256)} %constant.18.clone.1), kind=kCustom, calls=%fused_computation.6 | custom fusion | bytes 1049088 | tf_op jit(solution)/shard_map/scatter | solution.py:39
  23.3 4.1 %all-to-all-done.2 = bf16[16,2,16]{2,1,0:T(2,128)(2,1)S(1)} async-done(((bf16[16,2,16]{2,1,0:T(2,128)(2,1)}), bf16[16,2,16]{2,1,0:T(2,128)(2,1)S(1)}, u32[]{:S(2)}, u32[]{:S(2)}) %all-to-all-start.2) | async-done | bytes 1056 | tf_op jit(solution)/shard_map/all_to_all | solution.py:47
  27.4 0.1 reshape.196
  27.5 3.7 %all_to_all.20 = bf16[2,2,128]{2,1,0:T(2,128)(2,1)S(1)} all-to-all(bf16[2,2,128]{2,1,0:T(2,128)(2,1)S(1)} %reshape.196), channel_id=1, replica_groups=mesh['dp'=16,'grp'=2] {'grp'}, dimensions={0} | all-to-all | bytes 2048 | tf_op jit(solution)/shard_map/all_to_all | solution.py:50
  31.2 3.8 %all-to-all-start = ((bf16[16,2,16,1024]{3,2,1,0:T(8,128)(2,1)}), bf16[16,2,16,1024]{3,2,1,0:T(8,128)(2,1)S(1)}, u32[]{:S(2)}, u32[]{:S(2)}) async-start(bf16[16,2,16,1024]{3,2,1,0:T(8,128)(2,1)} %bitcast.1), calls=%async_computation | async-start | bytes 2097152 | tf_op jit(solution)/shard_map/all_to_all | solution.py:46
  35.1 0.6 select_reduce_fusion.1
  35.7 0.2 fusion.42
  35.9 0.2 fusion.43
  36.1 0.2 fusion.44
  36.3 0.2 fusion.45
  36.5 4.6 %all-reduce.1 = (f32[1]{0:T(128)}, f32[1,1024]{1,0:T(1,128)S(1)}, f32[1,1024]{1,0:T(1,128)S(1)}, f32[1,1024]{1,0:T(1,128)S(1)}, f32[1,1024]{1,0:T(1,128)S(1)}, /...) all-reduce(f32[1]{0:T(128)} %bitcast.5, ...), channel_id=1, replica_groups=mesh['dp'=16,'grp'=2] {'grp'}, use_global_device_ids=true, to_apply=%region_5.6 | all-reduce | flops 4104 | bytes 32832 | tf_op jit(solution)/shard_map/psum | solution.py:10
  41.1 82.4 %all-reduce = (f32[]{:T(128)}, bf16[1,1024]{1,0:T(2,128)(2,1)S(1)}, bf16[1,1024]{1,0:T(2,128)(2,1)S(1)}, bf16[1,1024]{1,0:T(2,128)(2,1)S(1)}, bf16[1,1024]{1,0:T...) all-reduce(f32[]{:T(128)} %bitcast.6, ...), channel_id=1, replica_groups=mesh['dp'=16,'grp'=2] {'dp'}, use_global_device_ids=true, to_apply=%region_6.7 | all-reduce | flops 4104 | bytes 24640 | tf_op jit(solution)/shard_map/psum | solution.py:11
  131.5 0.7 fusion.17
  144.0 0.1 copy.27
  144.1 4.6 %all_to_all.21 = bf16[16,2,16,1024]{3,2,0,1:T(8,128)(2,1)S(1)} all-to-all(bf16[16,2,16,1024]{3,2,0,1:T(8,128)(2,1)S(1)} %copy.27), channel_id=1, replica_groups=mesh['dp'=16,'grp'=2] {'grp'}, dimensions={1} | all-to-all | bytes 2097152 | tf_op jit(solution)/shard_map/all_to_all | solution.py:49
  148.7 0.1 copy.28
  148.8 0.4 fusion.29
  149.2 0.4 fusion.27
  149.6 0.4 fusion.25
  150.0 0.4 fusion.23
  150.4 0.3 fusion
  150.6 2.6 %convert_multiply_fusion.4 = (f32[16,2,16]{2,0,1:T(8,128)S(1)}, f32[16,2,16]{2,0,1:T(8,128)S(1)}, f32[16,2,16]{2,0,1:T(8,128)S(1)}, f32[16,2,16]{2,0,1:T(8,128)S(1)}, f32[16,2,16]{2,0,1:T(8,128)S(1)}) fusion(f32[]{:T(128)} %get-tuple-element.21, f32[]{:T(128)} %get-tuple-element.27, f32[]{:T(128)} %get-tuple-element.29, f32[]{:T(128)} %get-tuple-element.31, ...), kind=kLoop, calls=%fused_computation.12 | loop fusion | flops 5632 | bytes 13328 | tf_op jit(solution)/shard_map/mul | solution.py:105
  153.8 3.0 %multiply_subtract_fusion = (f32[512]{0:T(512)}, f32[512]{0:T(512)S(1)}, f32[512]{0:T(512)S(1)}, f32[512]{0:T(512)S(1)}, f32[512]{0:T(512)S(1)}) fusion(f32[512]{0:T(512)S(1)} %reshape.117, f32[]{:T(128)S(6)} %sqrt.15, f32[]{:T(128)S(6)} %div.115, f32[]{:T(128)S(6)} %div.113, f32[]{:T(128)S(6)} %div.111, f32[]{:T(128)} %get-tuple-element.32, s32[]{:T(128)S(6)} %mul.232, ...), kind=kLoop, calls=%fused_computation.64 | loop fusion | flops 23552 | bytes 28732 | tf_op jit(solution)/shard_map/sub | solution.py:108
  156.7 0.6 pad_maximum_fusion
  (28 shorter events, 0.7 us)
Async XLA Ops:
  11.8 15.6 %all-to-all-start.2 = ((bf16[16,2,16]{2,1,0:T(2,128)(2,1)}), bf16[16,2,16]{2,1,0:T(2,128)(2,1)S(1)}, u32[]{:S(2)}, u32[]{:S(2)}) async-start(bf16[16,2,16]{2,1,0:T(2,128)(2,1)} %reshape.113), calls=%async_computation.2 | async-start | bytes 16384 | tf_op jit(solution)/shard_map/all_to_all | solution.py:47
  31.2 4.5 %copy-start.1 = (bf16[256,1024]{1,0:T(8,128)(2,1)S(1)}, bf16[256,1024]{1,0:T(8,128)(2,1)}, u32[]{:S(2)}) copy-start(bf16[256,1024]{1,0:T(8,128)(2,1)} %param.7) | copy-start | bytes 1572868
  31.2 112.8 %all-to-all-start = ((bf16[16,2,16,1024]{3,2,1,0:T(8,128)(2,1)}), bf16[16,2,16,1024]{3,2,1,0:T(8,128)(2,1)S(1)}, u32[]{:S(2)}, u32[]{:S(2)}) async-start(bf16[16,2,16,1024]{3,2,1,0:T(8,128)(2,1)} %bitcast.1), calls=%async_computation | async-start | bytes 2097152 | tf_op jit(solution)/shard_map/all_to_all | solution.py:46
  148.8 1.2 copy-start
